TPU v7x, 32 devices: a whole 2x2x4 slice. The times are simulated.
32 devices in a mesh: section: 8 (over y, x, core), shard: 4 (over z).
Axes of the slice: x: 2, y: 2, z: 4, core: 2. Of those that a mesh axis runs over, the one named last changes fastest.
Arguments:
- kept_slab: bfloat16 [131072, 768], P(('section', 'shard')), may hold values from -1 to 1, as said below
- new_rows: bfloat16 [4, 256, 768], P(None, ('section', 'shard')), may hold values from -1 to 1, as said below
- append_mask: int32 [4, 256], P(None, ('section', 'shard')), may hold values 0 or 1
Outputs:
- maxima: float32 [4, 256], P(None, ('section', 'shard'))
Inputs may be any that keep to these rules, and one draw needn't show every extreme that they name: `kept_slab`: every row has unit Euclidean length up to bfloat16 rounding. `new_rows`: every row has unit Euclidean length up to bfloat16 rounding.
All inputs are finite; a program needn't handle non-finite values. No bound on the sum of `append_mask` on one device may be relied on, other than what follows from the above.
Results may differ from a plain program's by a relative error of at most 0.0003.
Values may be sent and summed in bfloat16 or wider, within the bound.
No kernel may reach another device: no remote copies, remote signals or barrier semaphores. Data moves between devices by JAX's collectives and lax.ppermute only.
A program may use at most 64 MiB of HBM per device.

v0:
```python
import jax
import jax.numpy as jnp
from jax import lax
from jax.sharding import PartitionSpec as P


def per_device(kept_slab, new_rows, append_mask):
    micro_count = new_rows.shape[0]
    own_count = new_rows.shape[1]
    width = new_rows.shape[2]
    devices_total = lax.axis_size("section") * lax.axis_size("shard")
    batch_rows = own_count * devices_total
    append_flags = append_mask.astype(jnp.bfloat16)
    gathered_rows, gathered_flags = (
        lax.all_gather(new_rows, ("section", "shard"), axis=1, tiled=True),
        lax.all_gather(append_flags, ("section", "shard"), axis=1, tiled=True),
    )
    flattened = gathered_rows.reshape(micro_count * batch_rows, width)
    slab_rows = kept_slab.shape[0]
    block_rows = min(512, slab_rows)
    kept_blocks = kept_slab.reshape(slab_rows // block_rows, block_rows, width)

    def visit(highest, block):
        scores = lax.dot_general(
            flattened, block, (((1,), (1,)), ((), ())), preferred_element_type=jnp.float32
        )
        return (jnp.maximum(highest, jnp.max(scores, axis=1)), None)

    slab_flat, _ = lax.scan(
        visit, jnp.full((micro_count * batch_rows,), -3.0, jnp.float32), kept_blocks
    )
    slab_state = slab_flat.reshape(micro_count, batch_rows)
    later = lax.broadcasted_iota(
        jnp.int32, (micro_count, 1, micro_count, 1), 0
    ) > lax.broadcasted_iota(jnp.int32, (micro_count, 1, micro_count, 1), 2)
    cross = jnp.einsum("qid,kjd->qikj", new_rows, gathered_rows, preferred_element_type=jnp.float32)
    usable = later & (gathered_flags[None, None, :, :] > 0.5)
    stream_state = jnp.max(jnp.where(usable, cross, jnp.float32(-3.0)), axis=(2, 3))
    received = lax.all_to_all(
        slab_state, ("section", "shard"), split_axis=1, concat_axis=0, tiled=True
    )
    own_slab = jnp.max(received.reshape(devices_total, micro_count, own_count), axis=0)
    return jnp.maximum(own_slab, stream_state)


def solution(mesh):
    return jax.shard_map(
        per_device,
        mesh=mesh,
        in_specs=(
            P(("section", "shard"), None),
            P(None, ("section", "shard"), None),
            P(None, ("section", "shard")),
        ),
        out_specs=P(None, ("section", "shard")),
        check_vma=False,
    )
```

profile of v0, /device:TPU:0, one launch (start us, length us, event | category | flops | bytes accessed | tf_op | source)
XLA Modules:
  0.0 118.4 jit_solution(1405508363463907266)
XLA Ops:
  6.5 0.0 all-gather.3.cloned.1.call-start
  6.5 0.7 all-gather.3.cloned.1.call-update
  7.3 0.7 convert_bitcast_fusion
  8.0 70.0 %all-gather = bf16[32,8,4]{1,2,0:T(4,128)(2,1)S(1)} all-gather(bf16[1,8,4]{1,2,0:T(4,128)(2,1)S(1)} %convert_bitcast_fusion), channel_id=1, replica_groups=mesh['section'=8,'shard'=4] {'section','shard'}, dimensions={0}, use_global_device_ids=true | all-gather | bytes 2112 | tf_op jit(solution)/shard_map/all_gather | solution.py:16
  78.0 0.1 copy.8
  78.1 0.1 copy.9
  78.2 0.1 reshape.34
  78.3 0.1 broadcast_and_fusion
  78.4 0.0 all-gather.3.cloned.1.call-done
  78.4 0.0 copy-start
  78.4 21.7 %while.11 = (s32[]{:T(128)}, f32[1024]{0:T(1024)S(1)}, bf16[8,512,768]{2,1,0:T(8,128)(2,1)}, bf16[1024,768]{1,0:T(8,128)(2,1)}, s32[]{:T(128)}, /*index=5*/s32[]{:T(128)}) while((s32[]{:T(128)}, f32[1024]{0:T(1024)S(1)}, bf16[8,512,768]{2,1,0:T(8,128)(2,1)}, bf16[1024,768]{1,0:T(8,128)(2,1)}, s32[]{:T(128)}, ...), condition=%wide.region_2.3_spmd.clone, body=%wide.region_0.2_spmd.clone.sunk | while | flops 805831680 | bytes 2375771 | solution.py:29
  78.4 2.7 %convolution_reduce_fusion.2 = f32[1024]{0:T(1024)S(1)} fusion(bf16[1024,768]{1,0:T(8,128)(2,1)} %get-tuple-element.91, bf16[8,512,768]{2,1,0:T(8,128)(2,1)} %get-tuple-element.90, s32[]{:T(128)S(6)} %copy.13), kind=kOutput, calls=%fused_computation.clone.1 | convolution fusion | flops 805829632 | bytes 2363396 | tf_op jit(solution)/shard_map/while/body/eval_jaxpr/dot_general | solution.py:24
  81.1 2.7 %convolution_reduce_fusion.2 = f32[1024]{0:T(1024)S(1)} fusion(bf16[1024,768]{1,0:T(8,128)(2,1)} %get-tuple-element.91, bf16[8,512,768]{2,1,0:T(8,128)(2,1)} %get-tuple-element.90, s32[]{:T(128)S(6)} %copy.13), kind=kOutput, calls=%fused_computation.clone.1 | convolution fusion | flops 805829632 | bytes 2363396 | tf_op jit(solution)/shard_map/while/body/eval_jaxpr/dot_general | solution.py:24
  83.9 2.7 %convolution_reduce_fusion.2 = f32[1024]{0:T(1024)S(1)} fusion(bf16[1024,768]{1,0:T(8,128)(2,1)} %get-tuple-element.91, bf16[8,512,768]{2,1,0:T(8,128)(2,1)} %get-tuple-element.90, s32[]{:T(128)S(6)} %copy.13), kind=kOutput, calls=%fused_computation.clone.1 | convolution fusion | flops 805829632 | bytes 2363396 | tf_op jit(solution)/shard_map/while/body/eval_jaxpr/dot_general | solution.py:24
  86.6 2.7 %convolution_reduce_fusion.2 = f32[1024]{0:T(1024)S(1)} fusion(bf16[1024,768]{1,0:T(8,128)(2,1)} %get-tuple-element.91, bf16[8,512,768]{2,1,0:T(8,128)(2,1)} %get-tuple-element.90, s32[]{:T(128)S(6)} %copy.13), kind=kOutput, calls=%fused_computation.clone.1 | convolution fusion | flops 805829632 | bytes 2363396 | tf_op jit(solution)/shard_map/while/body/eval_jaxpr/dot_general | solution.py:24
  89.3 2.7 %convolution_reduce_fusion.2 = f32[1024]{0:T(1024)S(1)} fusion(bf16[1024,768]{1,0:T(8,128)(2,1)} %get-tuple-element.91, bf16[8,512,768]{2,1,0:T(8,128)(2,1)} %get-tuple-element.90, s32[]{:T(128)S(6)} %copy.13), kind=kOutput, calls=%fused_computation.clone.1 | convolution fusion | flops 805829632 | bytes 2363396 | tf_op jit(solution)/shard_map/while/body/eval_jaxpr/dot_general | solution.py:24
  92.0 2.7 %convolution_reduce_fusion.2 = f32[1024]{0:T(1024)S(1)} fusion(bf16[1024,768]{1,0:T(8,128)(2,1)} %get-tuple-element.91, bf16[8,512,768]{2,1,0:T(8,128)(2,1)} %get-tuple-element.90, s32[]{:T(128)S(6)} %copy.13), kind=kOutput, calls=%fused_computation.clone.1 | convolution fusion | flops 805829632 | bytes 2363396 | tf_op jit(solution)/shard_map/while/body/eval_jaxpr/dot_general | solution.py:24
  94.7 2.7 %convolution_reduce_fusion.2 = f32[1024]{0:T(1024)S(1)} fusion(bf16[1024,768]{1,0:T(8,128)(2,1)} %get-tuple-element.91, bf16[8,512,768]{2,1,0:T(8,128)(2,1)} %get-tuple-element.90, s32[]{:T(128)S(6)} %copy.13), kind=kOutput, calls=%fused_computation.clone.1 | convolution fusion | flops 805829632 | bytes 2363396 | tf_op jit(solution)/shard_map/while/body/eval_jaxpr/dot_general | solution.py:24
  97.4 2.7 %convolution_reduce_fusion.2 = f32[1024]{0:T(1024)S(1)} fusion(bf16[1024,768]{1,0:T(8,128)(2,1)} %get-tuple-element.91, bf16[8,512,768]{2,1,0:T(8,128)(2,1)} %get-tuple-element.90, s32[]{:T(128)S(6)} %copy.13), kind=kOutput, calls=%fused_computation.clone.1 | convolution fusion | flops 805829632 | bytes 2363396 | tf_op jit(solution)/shard_map/while/body/eval_jaxpr/dot_general | solution.py:24
  100.1 0.1 all_to_all.10
  100.2 0.7 copy.7
  100.9 2.5 %all-to-all-start = ((f32[4,32,8]{2,0,1:T(4,128)}), f32[4,32,8]{2,0,1:T(4,128)S(1)}, u32[]{:S(2)}, u32[]{:S(2)}) async-start(f32[4,32,8]{2,0,1:T(4,128)} %copy.7), calls=%async_computation | async-start | bytes 131072 | tf_op jit(solution)/shard_map/all_to_all | solution.py:39
  103.4 0.0 copy-done
  103.4 2.1 %fusion.8 = f32[4,8]{1,0:T(4,128)S(1)} fusion(bf16[4,256,768]{2,1,0:T(8,128)(2,1)} %bitcast.30, pred[4,4,256]{2,1,0:T(4,128)(4,1)S(1)} %broadcast_and_fusion, bf16[4,8,768]{2,1,0:T(8,128)(2,1)S(1)} %copy-done), kind=kOutput, calls=%fused_computation.8 | convolution fusion | flops 50397152 | bytes 1626240 | tf_op jit(solution)/shard_map/qid,kjd->qikj/dot_general | solution.py:36
  105.5 5.4 %all-to-all-done = f32[4,32,8]{2,0,1:T(4,128)S(1)} async-done(((f32[4,32,8]{2,0,1:T(4,128)}), f32[4,32,8]{2,0,1:T(4,128)S(1)}, u32[]{:S(2)}, u32[]{:S(2)}) %all-to-all-start) | async-done | bytes 4128 | tf_op jit(solution)/shard_map/all_to_all | solution.py:39
  111.0 0.6 max.6
  (12 shorter events, 0.1 us)
Async XLA Ops:
  6.5 71.9 %all-gather.3.cloned.1.call-start = ((), (), s32[]{:S(2)}) async-start(), calls=%async_computation.1 | async-start | bytes 1622016 | tf_op jit(solution)/shard_map/all_gather | solution.py:15
  78.4 25.0 %copy-start = (bf16[4,8,768]{2,1,0:T(8,128)(2,1)S(1)}, bf16[4,8,768]{2,1,0:T(8,128)(2,1)}, u32[]{:S(2)}) copy-start(bf16[4,8,768]{2,1,0:T(8,128)(2,1)} %param.6) | copy-start | bytes 147460
  100.9 10.1 %all-to-all-start = ((f32[4,32,8]{2,0,1:T(4,128)}), f32[4,32,8]{2,0,1:T(4,128)S(1)}, u32[]{:S(2)}, u32[]{:S(2)}) async-start(f32[4,32,8]{2,0,1:T(4,128)} %copy.7), calls=%async_computation | async-start | bytes 131072 | tf_op jit(solution)/shard_map/all_to_all | solution.py:39
Sparse Core Ops, SparseCore 0:
  10.2 55.3 all-gather.2
where the time goes:
time: 119 us; the launch traced here: 118 us
  blocking collectives  70 us (59%)
  matrix products  23.5 us (20%)
  between operations  13.5 us (11%)
  waiting for transfers between devices  6.15 us (5%)
  starting transfers between devices  2.55 us (2%)
  other arithmetic  1.46 us (1%)
    all_gather x1, blocking collectives, per_device(): lax.all_gather(append_flags, ('section', 'shard'), axis=1, tiled=True)  70 us
    dot_general x8, matrix products, visit(): lax.dot_general(flattened, block, (((1,), (1,)), ((), ())), preferred_ele...  21.4 us
    all_to_all x1, waiting for transfers between devices, per_device(): lax.all_to_all(slab_state, ('section', 'shard'), split_axis=1, concat_axi...  5.44 us
    all_to_all x1, starting transfers between devices, per_device(): lax.all_to_all(slab_state, ('section', 'shard'), split_axis=1, concat_axi...  2.55 us
  transfers between devices with their start and end apart: 2, of which 1 were waited for; matrix products, arithmetic and copies ran while one was open for 3% of the time, Pallas kernels for 0%

commit v1 on v0

--- a/solution.py
+++ b/solution.py
@@ -36,8 +36,14 @@
     cross = jnp.einsum("qid,kjd->qikj", new_rows, gathered_rows, preferred_element_type=jnp.float32)
     usable = later & (gathered_flags[None, None, :, :] > 0.5)
     stream_state = jnp.max(jnp.where(usable, cross, jnp.float32(-3.0)), axis=(2, 3))
-    received = lax.all_to_all(
-        slab_state, ("section", "shard"), split_axis=1, concat_axis=0, tiled=True
+    received = jnp.concatenate(
+        lax.all_to_all(
+            jnp.stack(jnp.split(slab_state, lax.axis_size(("section", "shard")), axis=1)),
+            ("section", "shard"),
+            0,
+            0,
+        ),
+        axis=0,
     )
     own_slab = jnp.max(received.reshape(devices_total, micro_count, own_count), axis=0)
     return jnp.maximum(own_slab, stream_state)

time: 119 us -> 139 us (1.17)
  local copies, waits for them, and re-layouts: 1.05 us -> 21 us
    unnamed x2 -> x33, local copies, waits for them, and re-layouts: 0.01 us -> 20.1 us
  transfers between devices with their start and end apart: 2 -> 2, of which waited for: 1 -> 1; matrix products, arithmetic and copies ran while one was open for 3% -> 2% of each run, Pallas kernels for 0% -> 0%
where the time goes in v1:
time: 139 us; the launch traced here: 138 us
  blocking collectives  70 us (50%)
  matrix products  23.4 us (17%)
  local copies, waits for them, and re-layouts  21 us (15%)
  between operations  13.5 us (10%)
  waiting for transfers between devices  6.15 us (4%)
  starting transfers between devices  2.55 us (2%)
  other arithmetic  1.46 us (1%)
    all_gather x1, blocking collectives, per_device(): lax.all_gather(append_flags, ('section', 'shard'), axis=1, tiled=True)  70 us
    dot_general x8, matrix products, visit(): lax.dot_general(flattened, block, (((1,), (1,)), ((), ())), preferred_ele...  21.4 us
    unnamed x33, local copies, waits for them, and re-layouts  20.1 us
    all_to_all x1, waiting for transfers between devices, per_device(): lax.all_to_all(jnp.stack(jnp.split(slab_state, lax.axis_size(('section',...  5.44 us
  transfers between devices with their start and end apart: 2, of which 1 were waited for; matrix products, arithmetic and copies ran while one was open for 2% of the time, Pallas kernels for 0%

profile of v1, /device:TPU:0, one launch (start us, length us, event | category | flops | bytes accessed | tf_op | source)
XLA Modules:
  0.0 138.4 jit_solution(10985815510101138703)
XLA Ops:
  6.5 0.0 all-gather.3.cloned.1.call-start
  6.5 0.7 all-gather.3.cloned.1.call-update
  7.3 0.7 convert_bitcast_fusion
  8.0 70.0 %all-gather = bf16[32,8,4]{1,2,0:T(4,128)(2,1)S(1)} all-gather(bf16[1,8,4]{1,2,0:T(4,128)(2,1)S(1)} %convert_bitcast_fusion), channel_id=1, replica_groups=mesh['section'=8,'shard'=4] {'section','shard'}, dimensions={0}, use_global_device_ids=true | all-gather | bytes 2112 | tf_op jit(solution)/shard_map/all_gather | solution.py:16
  78.0 0.1 copy.73
  78.1 0.1 copy.74
  78.2 0.1 reshape.31
  78.3 0.1 broadcast_and_fusion
  78.4 0.0 all-gather.3.cloned.1.call-done
  78.4 0.0 copy-start
  78.4 21.7 %while.11 = (s32[]{:T(128)}, f32[1024]{0:T(1024)S(1)}, bf16[8,512,768]{2,1,0:T(8,128)(2,1)}, bf16[1024,768]{1,0:T(8,128)(2,1)}, s32[]{:T(128)}, /*index=5*/s32[]{:T(128)}) while((s32[]{:T(128)}, f32[1024]{0:T(1024)S(1)}, bf16[8,512,768]{2,1,0:T(8,128)(2,1)}, bf16[1024,768]{1,0:T(8,128)(2,1)}, s32[]{:T(128)}, ...), condition=%wide.region_2.3_spmd.clone, body=%wide.region_0.2_spmd.clone.sunk | while | flops 805831680 | bytes 2375771 | solution.py:29
  78.4 2.7 %convolution_reduce_fusion.2 = f32[1024]{0:T(1024)S(1)} fusion(bf16[1024,768]{1,0:T(8,128)(2,1)} %get-tuple-element.91, bf16[8,512,768]{2,1,0:T(8,128)(2,1)} %get-tuple-element.90, s32[]{:T(128)S(6)} %copy.78), kind=kOutput, calls=%fused_computation.clone.1 | convolution fusion | flops 805829632 | bytes 2363396 | tf_op jit(solution)/shard_map/while/body/eval_jaxpr/dot_general | solution.py:24
  81.1 2.7 %convolution_reduce_fusion.2 = f32[1024]{0:T(1024)S(1)} fusion(bf16[1024,768]{1,0:T(8,128)(2,1)} %get-tuple-element.91, bf16[8,512,768]{2,1,0:T(8,128)(2,1)} %get-tuple-element.90, s32[]{:T(128)S(6)} %copy.78), kind=kOutput, calls=%fused_computation.clone.1 | convolution fusion | flops 805829632 | bytes 2363396 | tf_op jit(solution)/shard_map/while/body/eval_jaxpr/dot_general | solution.py:24
  83.9 2.7 %convolution_reduce_fusion.2 = f32[1024]{0:T(1024)S(1)} fusion(bf16[1024,768]{1,0:T(8,128)(2,1)} %get-tuple-element.91, bf16[8,512,768]{2,1,0:T(8,128)(2,1)} %get-tuple-element.90, s32[]{:T(128)S(6)} %copy.78), kind=kOutput, calls=%fused_computation.clone.1 | convolution fusion | flops 805829632 | bytes 2363396 | tf_op jit(solution)/shard_map/while/body/eval_jaxpr/dot_general | solution.py:24
  86.6 2.7 %convolution_reduce_fusion.2 = f32[1024]{0:T(1024)S(1)} fusion(bf16[1024,768]{1,0:T(8,128)(2,1)} %get-tuple-element.91, bf16[8,512,768]{2,1,0:T(8,128)(2,1)} %get-tuple-element.90, s32[]{:T(128)S(6)} %copy.78), kind=kOutput, calls=%fused_computation.clone.1 | convolution fusion | flops 805829632 | bytes 2363396 | tf_op jit(solution)/shard_map/while/body/eval_jaxpr/dot_general | solution.py:24
  89.3 2.7 %convolution_reduce_fusion.2 = f32[1024]{0:T(1024)S(1)} fusion(bf16[1024,768]{1,0:T(8,128)(2,1)} %get-tuple-element.91, bf16[8,512,768]{2,1,0:T(8,128)(2,1)} %get-tuple-element.90, s32[]{:T(128)S(6)} %copy.78), kind=kOutput, calls=%fused_computation.clone.1 | convolution fusion | flops 805829632 | bytes 2363396 | tf_op jit(solution)/shard_map/while/body/eval_jaxpr/dot_general | solution.py:24
  92.0 2.7 %convolution_reduce_fusion.2 = f32[1024]{0:T(1024)S(1)} fusion(bf16[1024,768]{1,0:T(8,128)(2,1)} %get-tuple-element.91, bf16[8,512,768]{2,1,0:T(8,128)(2,1)} %get-tuple-element.90, s32[]{:T(128)S(6)} %copy.78), kind=kOutput, calls=%fused_computation.clone.1 | convolution fusion | flops 805829632 | bytes 2363396 | tf_op jit(solution)/shard_map/while/body/eval_jaxpr/dot_general | solution.py:24
  94.7 2.7 %convolution_reduce_fusion.2 = f32[1024]{0:T(1024)S(1)} fusion(bf16[1024,768]{1,0:T(8,128)(2,1)} %get-tuple-element.91, bf16[8,512,768]{2,1,0:T(8,128)(2,1)} %get-tuple-element.90, s32[]{:T(128)S(6)} %copy.78), kind=kOutput, calls=%fused_computation.clone.1 | convolution fusion | flops 805829632 | bytes 2363396 | tf_op jit(solution)/shard_map/while/body/eval_jaxpr/dot_general | solution.py:24
  97.4 2.7 %convolution_reduce_fusion.2 = f32[1024]{0:T(1024)S(1)} fusion(bf16[1024,768]{1,0:T(8,128)(2,1)} %get-tuple-element.91, bf16[8,512,768]{2,1,0:T(8,128)(2,1)} %get-tuple-element.90, s32[]{:T(128)S(6)} %copy.78), kind=kOutput, calls=%fused_computation.clone.1 | convolution fusion | flops 805829632 | bytes 2363396 | tf_op jit(solution)/shard_map/while/body/eval_jaxpr/dot_general | solution.py:24
  100.1 0.6 constant_dynamic-update-slice_fusion.31
  100.7 0.7 constant_dynamic-update-slice_fusion.30
  101.4 0.6 constant_dynamic-update-slice_fusion.29
  102.0 0.7 constant_dynamic-update-slice_fusion.28
  102.7 0.7 constant_dynamic-update-slice_fusion.27
  103.3 0.6 constant_dynamic-update-slice_fusion.26
  104.0 0.7 constant_dynamic-update-slice_fusion.25
  104.7 0.6 constant_dynamic-update-slice_fusion.24
  105.3 0.6 constant_dynamic-update-slice_fusion.23
  105.9 0.7 constant_dynamic-update-slice_fusion.22
  106.6 0.6 constant_dynamic-update-slice_fusion.21
  107.3 0.7 constant_dynamic-update-slice_fusion.20
  107.9 0.7 constant_dynamic-update-slice_fusion.19
  108.6 0.6 constant_dynamic-update-slice_fusion.18
  109.2 0.7 constant_dynamic-update-slice_fusion.17
  109.9 0.6 constant_dynamic-update-slice_fusion.16
  110.5 0.6 constant_dynamic-update-slice_fusion.15
  111.1 0.7 constant_dynamic-update-slice_fusion.14
  111.7 0.6 constant_dynamic-update-slice_fusion.13
  112.4 0.7 constant_dynamic-update-slice_fusion.12
  113.0 0.7 constant_dynamic-update-slice_fusion.11
  113.7 0.6 constant_dynamic-update-slice_fusion.10
  114.3 0.7 constant_dynamic-update-slice_fusion.9
  115.0 0.6 constant_dynamic-update-slice_fusion.8
  115.6 0.6 constant_dynamic-update-slice_fusion.7
  116.3 0.7 constant_dynamic-update-slice_fusion.6
  117.0 0.6 constant_dynamic-update-slice_fusion.5
  117.6 0.7 constant_dynamic-update-slice_fusion.4
  118.3 0.7 constant_dynamic-update-slice_fusion.3
  118.9 0.6 constant_dynamic-update-slice_fusion.2
  119.6 0.7 constant_dynamic-update-slice_fusion.1
  120.2 0.6 constant_dynamic-update-slice_fusion
  120.9 2.5 %all-to-all-start = ((f32[32,4,8]{2,1,0:T(4,128)}), f32[32,4,8]{2,1,0:T(4,128)S(1)}, u32[]{:S(2)}, u32[]{:S(2)}) async-start(f32[32,4,8]{2,1,0:T(4,128)} %constant_dynamic-update-slice_fusion), calls=%async_computation | async-start | bytes 131072 | tf_op jit(solution)/shard_map/all_to_all | solution.py:40
  123.4 0.0 copy-done
  123.4 2.0 %fusion.8 = f32[4,8]{1,0:T(4,128)S(1)} fusion(bf16[4,256,768]{2,1,0:T(8,128)(2,1)} %bitcast.158, pred[4,4,256]{2,1,0:T(4,128)(4,1)S(1)} %broadcast_and_fusion, bf16[4,8,768]{2,1,0:T(8,128)(2,1)S(1)} %copy-done), kind=kOutput, calls=%fused_computation.8 | convolution fusion | flops 50397152 | bytes 1626240 | tf_op jit(solution)/shard_map/qid,kjd->qikj/dot_general | solution.py:36
  125.5 5.4 %all-to-all-done = f32[32,4,8]{2,1,0:T(4,128)S(1)} async-done(((f32[32,4,8]{2,1,0:T(4,128)}), f32[32,4,8]{2,1,0:T(4,128)S(1)}, u32[]{:S(2)}, u32[]{:S(2)}) %all-to-all-start) | async-done | bytes 4128 | tf_op jit(solution)/shard_map/all_to_all | solution.py:40
  131.0 0.6 max.6
  (13 shorter events, 0.1 us)
Async XLA Ops:
  6.5 71.9 %all-gather.3.cloned.1.call-start = ((), (), s32[]{:S(2)}) async-start(), calls=%async_computation.1 | async-start | bytes 1622016 | tf_op jit(solution)/shard_map/all_gather | solution.py:15
  78.4 45.0 %copy-start = (bf16[4,8,768]{2,1,0:T(8,128)(2,1)S(1)}, bf16[4,8,768]{2,1,0:T(8,128)(2,1)}, u32[]{:S(2)}) copy-start(bf16[4,8,768]{2,1,0:T(8,128)(2,1)} %param.6) | copy-start | bytes 147460
  120.9 10.1 %all-to-all-start = ((f32[32,4,8]{2,1,0:T(4,128)}), f32[32,4,8]{2,1,0:T(4,128)S(1)}, u32[]{:S(2)}, u32[]{:S(2)}) async-start(f32[32,4,8]{2,1,0:T(4,128)} %constant_dynamic-update-slice_fusion), calls=%async_computation | async-start | bytes 131072 | tf_op jit(solution)/shard_map/all_to_all | solution.py:40
Sparse Core Ops, SparseCore 0:
  10.2 55.3 all-gather.2
